TPU v7x, 256 devices: a whole 4x4x8 slice. The times are simulated.
256 devices in a mesh: leaf: 32 (over x, y, core), front: 8 (over z).
Axes of the slice: x: 4, y: 4, z: 8, core: 2. Of those that a mesh axis runs over, the one named last changes fastest.
Arguments:
- child_updates: float32 [32768, 1024], P('leaf', 'front'), as said below
- initial_one: float32 [32768, 2048], P('leaf', 'front'), as said below
- initial_two: float32 [16384, 2048], P('leaf', 'front'), as said below
- pattern_one: int32 [16, 16, 16], replicated, may hold values 0 or 1
- pattern_two: int32 [8, 16, 16], replicated, may hold values 0 or 1
- parent_map_one: int32 [16, 2, 16], replicated, may hold values from 0 to 15, each once within a row
- parent_map_two: int32 [8, 2, 16], replicated, may hold values from 0 to 15, each once within a row
Outputs:
- factor_one: float32 [32768, 1024], P('leaf', 'front')
- factor_two: float32 [16384, 1024], P('leaf', 'front')
- schur_two: float32 [8192, 1024], P('leaf', 'front')
Inputs may be any that keep to these rules, and one draw needn't show every extreme that they name: `parent_map_one`: each row is a permutation of 0 to 15; only its first 8 entries are used. `parent_map_two`: each row is a permutation of 0 to 15; only its first 8 entries are used. `initial_one`: each 2048 x 2048 front block is symmetric, and positive definite after any symmetric block mask. `initial_two`: each 2048 x 2048 front block is symmetric, and positive definite after any symmetric block mask. `child_updates`: each 1024 x 1024 matrix is symmetric positive definite.
All inputs are finite; a program needn't handle non-finite values.
Results may differ from a plain program's by a relative error of at most 0.0003.
Values sent between devices are 32-bit elements; how exact they have to be, the bound alone decides.
No kernel may reach another device: no remote copies, remote signals or barrier semaphores. Data moves between devices by JAX's collectives and lax.ppermute only.
A program may use at most 128 MiB of HBM per device.

v0:
```python
import jax
import jax.numpy as jnp
from jax import lax
from jax.sharding import PartitionSpec as P

BLK = 128
SEP = 1024
UPD = 1024
FR = 2048
HIGHEST = lax.Precision.HIGHEST


def swapped(block, axis, stride):
    count = lax.axis_size(axis)
    route = []
    for low in range(count):
        high = low | 1 << stride
        if high != low and high < count:
            route += [(low, high), (high, low)]
    return lax.ppermute(block, axis, route)


def spread(block, axis, holder):
    block = jnp.where(lax.axis_index(axis) == holder, block, jnp.zeros_like(block))
    return lax.psum(block, axis)


def solve_rows(chol_block, right_side):
    return jax.scipy.linalg.solve_triangular(chol_block, right_side.T, lower=True).T


def gather_subcube(pieces, level_depth, leaf_index):
    for bit_number in range(level_depth):
        partner = swapped(pieces, "leaf", bit_number)
        upper_half = leaf_index >> bit_number & 1 == 1
        pieces = jnp.where(
            upper_half, jnp.concatenate([partner, pieces], 0), jnp.concatenate([pieces, partner], 0)
        )
    return pieces


def fetch_rows(pieces, wanted, level_depth, leaf_index):
    columns = pieces.shape[1]
    full_panel = gather_subcube(pieces, level_depth, leaf_index)
    return jnp.take(full_panel.reshape(FR // BLK, BLK, columns), wanted, axis=0).reshape(
        wanted.shape[0] * BLK, columns
    )


def merge_halves(placed, level_depth, leaf_index):
    for bit_number in reversed(range(level_depth)):
        middle = placed.shape[0] // 2
        upper_half = leaf_index >> bit_number & 1 == 1
        kept_half = jnp.where(upper_half, placed[middle:], placed[:middle])
        given_half = jnp.where(upper_half, placed[:middle], placed[middle:])
        placed = kept_half + swapped(given_half, "leaf", bit_number)
    return placed


def assemble(
    child_tile, initial, pattern, parent_map, level_depth, leaf_index, front_index, col_blocks
):
    group_share = 2**level_depth
    child_share = group_share // 2
    front_group = leaf_index // group_share
    child_side = leaf_index // child_share % 2
    child_sub = leaf_index % child_share
    sub_index = leaf_index % group_share
    update_blocks = UPD // BLK
    front_blocks = FR // BLK
    tile_cols = 2 * col_blocks * BLK
    gathered = lax.all_gather(child_tile, "front", axis=1, tiled=True)
    child_rows = gathered.shape[0]
    child_row_blocks = child_rows // BLK
    both_maps = lax.dynamic_index_in_dim(parent_map, front_group, 0, keepdims=False)
    block_map = lax.dynamic_index_in_dim(both_maps, child_side, 0, keepdims=False)[:update_blocks]
    target_cols = 2 * col_blocks * front_index + jnp.arange(2 * col_blocks, dtype=jnp.int32)
    col_pick = (block_map[:, None] == target_cols[None, :]).astype(jnp.float32)
    picked = jnp.einsum(
        "rik,it->rtk", gathered.reshape(child_rows, update_blocks, BLK), col_pick, precision=HIGHEST
    )
    my_map = lax.dynamic_slice_in_dim(block_map, child_sub * child_row_blocks, child_row_blocks)
    row_place = (jnp.arange(front_blocks, dtype=jnp.int32)[:, None] == my_map[None, :]).astype(
        jnp.float32
    )
    placed = jnp.einsum(
        "ba,akc->bkc",
        row_place,
        picked.reshape(child_row_blocks, BLK, tile_cols),
        precision=HIGHEST,
    ).reshape(FR, tile_cols)
    merged = merge_halves(placed, level_depth, leaf_index)
    own_blocks = front_blocks // group_share
    whole_pattern = lax.dynamic_index_in_dim(pattern, front_group, 0, keepdims=False)
    row_part = lax.dynamic_slice_in_dim(whole_pattern, sub_index * own_blocks, own_blocks, 0)
    row_part = lax.dynamic_slice_in_dim(row_part, 2 * col_blocks * front_index, 2 * col_blocks, 1)
    col_part = lax.dynamic_slice_in_dim(
        whole_pattern, 2 * col_blocks * front_index, 2 * col_blocks, 0
    )
    col_part = lax.dynamic_slice_in_dim(col_part, sub_index * own_blocks, own_blocks, 1)
    row_ids = sub_index * own_blocks + jnp.arange(own_blocks, dtype=jnp.int32)
    keep_blocks = (row_part == 1) | (col_part.T == 1) | (row_ids[:, None] == target_cols[None, :])
    keep_mask = (
        jnp.broadcast_to(keep_blocks[:, None, :, None], (own_blocks, BLK, 2 * col_blocks, BLK))
        .reshape(own_blocks * BLK, tile_cols)
        .astype(jnp.float32)
    )
    return (initial * keep_mask + merged, row_ids, target_cols)


def factor_panels(
    front_tile, row_ids, target_cols, level_depth, leaf_index, front_index, col_blocks
):
    tile_rows = front_tile.shape[0]
    panel_width = col_blocks * BLK
    row_odd = jnp.repeat(row_ids % 2 == 1, BLK)
    row_sep = jnp.repeat(row_ids // 2, BLK)
    col_odd = jnp.repeat(target_cols % 2 == 1, BLK)
    col_sep = jnp.repeat(target_cols // 2, BLK)
    factor_tile = jnp.zeros((tile_rows, col_blocks, BLK), jnp.float32)
    for step_index in range(lax.axis_size("front")):
        first_block = step_index * col_blocks
        panel_slots = first_block + jnp.arange(col_blocks, dtype=jnp.int32)
        sep_cols = front_tile.reshape(tile_rows, 2 * col_blocks, BLK)[:, 0::2].reshape(
            tile_rows, panel_width
        )
        panel_rows = spread(sep_cols, "front", step_index)
        wanted = jnp.concatenate([2 * panel_slots, target_cols])
        fetched = fetch_rows(panel_rows, wanted, level_depth, leaf_index)
        chol_block = jnp.linalg.cholesky(fetched[:panel_width])
        own_factor = solve_rows(chol_block, panel_rows)
        col_factor = solve_rows(chol_block, fetched[panel_width:])
        own_keep = (row_odd | (row_sep >= first_block + col_blocks)).astype(jnp.float32)
        col_keep = (col_odd | (col_sep >= first_block + col_blocks)).astype(jnp.float32)
        front_tile = front_tile - jnp.dot(
            own_factor * own_keep[:, None], (col_factor * col_keep[:, None]).T, precision=HIGHEST
        )
        valid_rows = (row_odd[:, None] | (row_sep[:, None] >= panel_slots[None, :])).astype(
            jnp.float32
        )
        factor_tile = jnp.where(
            front_index == step_index,
            own_factor.reshape(tile_rows, col_blocks, BLK) * valid_rows[:, :, None],
            factor_tile,
        )
    schur_tile = front_tile.reshape(tile_rows // BLK, BLK, 2 * col_blocks, BLK)[
        1::2, :, 1::2, :
    ].reshape(tile_rows // 2, col_blocks * BLK)
    return (factor_tile.reshape(tile_rows, col_blocks * BLK), schur_tile)


def per_device(
    child_updates,
    initial_one,
    initial_two,
    pattern_one,
    pattern_two,
    parent_map_one,
    parent_map_two,
):
    leaf_index = lax.axis_index("leaf")
    front_index = lax.axis_index("front")
    col_blocks = SEP // BLK // lax.axis_size("front")
    child_tile = child_updates
    factors = []
    for level_depth, initial, pattern, parent_map in (
        (1, initial_one, pattern_one, parent_map_one),
        (2, initial_two, pattern_two, parent_map_two),
    ):
        front_tile, row_ids, target_cols = assemble(
            child_tile,
            initial,
            pattern,
            parent_map,
            level_depth,
            leaf_index,
            front_index,
            col_blocks,
        )
        factor_tile, child_tile = factor_panels(
            front_tile, row_ids, target_cols, level_depth, leaf_index, front_index, col_blocks
        )
        factors.append(factor_tile)
    return (factors[0], factors[1], child_tile)


def solution(mesh):
    placed = (P("leaf", "front"), P("leaf", "front"), P("leaf", "front"), P(), P(), P(), P())
    return jax.shard_map(
        per_device,
        mesh=mesh,
        in_specs=placed,
        out_specs=(P("leaf", "front"), P("leaf", "front"), P("leaf", "front")),
        check_vma=False,
    )
```

profile of v0, /device:TPU:1, one launch (start us, length us, event | category | flops | bytes accessed | tf_op | source)
XLA Modules:
  0.0 1970.0 jit_solution(7487446941033398264)
XLA Ops:
  8.1 65.2 %all-gather.3.cloned.1.call-done = f32[1024,1024]{1,0:T(8,128)} async-done(((f32[1024,128]{1,0:T(8,128)}), f32[1024,1024]{1,0:T(8,128)}) %all-gather.3.cloned.1.call-update) | async-done | bytes 4194320 | tf_op jit(solution)/shard_map/all_gather | solution.py:72
  96.0 64.8 %all-reduce.17.cloned.1.call-done = f32[1024,128]{0,1:T(8,128)} async-done(((f32[1024,128]{0,1:T(8,128)}), f32[1024,128]{0,1:T(8,128)}) %all-reduce.17.cloned.1.call-update) | async-done | bytes 524304 | tf_op jit(solution)/shard_map/psum | solution.py:25
  198.7 67.0 %all-reduce.19.cloned.1.call-done = f32[1024,128]{0,1:T(8,128)} async-done(((f32[1024,128]{0,1:T(8,128)}), f32[1024,128]{0,1:T(8,128)}) %all-reduce.19.cloned.1.call-update) | async-done | bytes 524304 | tf_op jit(solution)/shard_map/psum | solution.py:25
  303.9 67.0 %all-reduce.21.cloned.1.call-done = f32[1024,128]{0,1:T(8,128)} async-done(((f32[1024,128]{0,1:T(8,128)}), f32[1024,128]{0,1:T(8,128)}) %all-reduce.21.cloned.1.call-update) | async-done | bytes 524304 | tf_op jit(solution)/shard_map/psum | solution.py:25
  408.9 67.0 %all-reduce.23.cloned.1.call-done = f32[1024,128]{0,1:T(8,128)} async-done(((f32[1024,128]{0,1:T(8,128)}), f32[1024,128]{0,1:T(8,128)}) %all-reduce.23.cloned.1.call-update) | async-done | bytes 524304 | tf_op jit(solution)/shard_map/psum | solution.py:25
  513.9 67.0 %all-reduce.25.cloned.1.call-done = f32[1024,128]{0,1:T(8,128)} async-done(((f32[1024,128]{0,1:T(8,128)}), f32[1024,128]{0,1:T(8,128)}) %all-reduce.25.cloned.1.call-update) | async-done | bytes 524304 | tf_op jit(solution)/shard_map/psum | solution.py:25
  619.1 67.0 %all-reduce.27.cloned.1.call-done = f32[1024,128]{0,1:T(8,128)} async-done(((f32[1024,128]{0,1:T(8,128)}), f32[1024,128]{0,1:T(8,128)}) %all-reduce.27.cloned.1.call-update) | async-done | bytes 524304 | tf_op jit(solution)/shard_map/psum | solution.py:25
  724.3 67.1 %all-reduce.29.cloned.1.call-done = f32[1024,128]{0,1:T(8,128)} async-done(((f32[1024,128]{0,1:T(8,128)}), f32[1024,128]{0,1:T(8,128)}) %all-reduce.29.cloned.1.call-update) | async-done | bytes 524304 | tf_op jit(solution)/shard_map/psum | solution.py:25
  829.3 67.1 %all-reduce.31.cloned.1.call-done = f32[1024,128]{0,1:T(8,128)} async-done(((f32[1024,128]{0,1:T(8,128)}), f32[1024,128]{0,1:T(8,128)}) %all-reduce.31.cloned.1.call-update) | async-done | bytes 524304 | tf_op jit(solution)/shard_map/psum | solution.py:25
  936.3 40.7 %all-gather.5.cloned.1.call-done = f32[512,1024]{1,0:T(8,128)} async-done(((f32[512,128]{1,0:T(8,128)}), f32[512,1024]{1,0:T(8,128)}) %all-gather.5.cloned.1.call-update) | async-done | bytes 2097168 | tf_op jit(solution)/shard_map/all_gather | solution.py:72
  987.9 15.9 collective-permute-done.9
  1016.5 65.7 %all-reduce.33.cloned.1.call-done = f32[512,128]{0,1:T(8,128)} async-done(((f32[512,128]{0,1:T(8,128)}), f32[512,128]{0,1:T(8,128)}) %all-reduce.33.cloned.1.call-update) | async-done | bytes 262160 | tf_op jit(solution)/shard_map/psum | solution.py:25
  1091.7 11.8 collective-permute-done.12
  1132.3 67.0 %all-reduce.35.cloned.1.call-done = f32[512,128]{0,1:T(8,128)} async-done(((f32[512,128]{0,1:T(8,128)}), f32[512,128]{0,1:T(8,128)}) %all-reduce.35.cloned.1.call-update) | async-done | bytes 262160 | tf_op jit(solution)/shard_map/psum | solution.py:25
  1208.6 11.8 collective-permute-done.14
  1249.3 67.1 %all-reduce.37.cloned.1.call-done = f32[512,128]{0,1:T(8,128)} async-done(((f32[512,128]{0,1:T(8,128)}), f32[512,128]{0,1:T(8,128)}) %all-reduce.37.cloned.1.call-update) | async-done | bytes 262160 | tf_op jit(solution)/shard_map/psum | solution.py:25
  1366.4 67.0 %all-reduce.39.cloned.1.call-done = f32[512,128]{0,1:T(8,128)} async-done(((f32[512,128]{0,1:T(8,128)}), f32[512,128]{0,1:T(8,128)}) %all-reduce.39.cloned.1.call-update) | async-done | bytes 262160 | tf_op jit(solution)/shard_map/psum | solution.py:25
  1442.7 11.8 collective-permute-done.18
  1483.5 67.0 %all-reduce.41.cloned.1.call-done = f32[512,128]{0,1:T(8,128)} async-done(((f32[512,128]{0,1:T(8,128)}), f32[512,128]{0,1:T(8,128)}) %all-reduce.41.cloned.1.call-update) | async-done | bytes 262160 | tf_op jit(solution)/shard_map/psum | solution.py:25
  1560.0 11.8 collective-permute-done.20
  1600.8 67.0 %all-reduce.43.cloned.1.call-done = f32[512,128]{0,1:T(8,128)} async-done(((f32[512,128]{0,1:T(8,128)}), f32[512,128]{0,1:T(8,128)}) %all-reduce.43.cloned.1.call-update) | async-done | bytes 262160 | tf_op jit(solution)/shard_map/psum | solution.py:25
  1677.0 11.8 collective-permute-done.22
  1718.5 67.0 %all-reduce.45.cloned.1.call-done = f32[512,128]{0,1:T(8,128)} async-done(((f32[512,128]{0,1:T(8,128)}), f32[512,128]{0,1:T(8,128)}) %all-reduce.45.cloned.1.call-update) | async-done | bytes 262160 | tf_op jit(solution)/shard_map/psum | solution.py:25
  1840.7 67.0 %all-reduce.47.cloned.1.call-done = f32[512,128]{0,1:T(8,128)} async-done(((f32[512,128]{0,1:T(8,128)}), f32[512,128]{0,1:T(8,128)}) %all-reduce.47.cloned.1.call-update) | async-done | bytes 262160 | tf_op jit(solution)/shard_map/psum | solution.py:25
  (641 shorter events, 702.4 us)
Async XLA Ops:
  7.2 66.1 %all-gather.3.cloned.1.call-start = ((), (), s32[]{:S(2)}) async-start(), calls=%async_computation | async-start | bytes 4718592 | tf_op jit(solution)/shard_map/all_gather | solution.py:72
  7.9 152.8 %all-reduce.17.cloned.1.call-start = ((), (), s32[]{:S(2)}) async-start(), calls=%async_computation.1 | async-start | bytes 1048576 | tf_op jit(solution)/shard_map/psum | solution.py:25
  95.8 169.9 %all-reduce.19.cloned.1.call-start = ((), (), s32[]{:S(2)}) async-start(), calls=%async_computation.2 | async-start | bytes 1048576 | tf_op jit(solution)/shard_map/psum | solution.py:25
  198.6 172.3 %all-reduce.21.cloned.1.call-start = ((), (), s32[]{:S(2)}) async-start(), calls=%async_computation.3 | async-start | bytes 1048576 | tf_op jit(solution)/shard_map/psum | solution.py:25
  303.8 172.1 %all-reduce.23.cloned.1.call-start = ((), (), s32[]{:S(2)}) async-start(), calls=%async_computation.4 | async-start | bytes 1048576 | tf_op jit(solution)/shard_map/psum | solution.py:25
  408.7 172.2 %all-reduce.25.cloned.1.call-start = ((), (), s32[]{:S(2)}) async-start(), calls=%async_computation.5 | async-start | bytes 1048576 | tf_op jit(solution)/shard_map/psum | solution.py:25
  513.9 172.2 %all-reduce.27.cloned.1.call-start = ((), (), s32[]{:S(2)}) async-start(), calls=%async_computation.6 | async-start | bytes 1048576 | tf_op jit(solution)/shard_map/psum | solution.py:25
  619.0 172.4 %all-reduce.29.cloned.1.call-start = ((), (), s32[]{:S(2)}) async-start(), calls=%async_computation.7 | async-start | bytes 1048576 | tf_op jit(solution)/shard_map/psum | solution.py:25
  724.2 172.1 %all-reduce.31.cloned.1.call-start = ((), (), s32[]{:S(2)}) async-start(), calls=%async_computation.8 | async-start | bytes 1048576 | tf_op jit(solution)/shard_map/psum | solution.py:25
  829.2 147.8 %all-gather.5.cloned.1.call-start = ((), (), s32[]{:S(2)}) async-start(), calls=%async_computation.9 | async-start | bytes 2359296 | tf_op jit(solution)/shard_map/all_gather | solution.py:72
  935.2 147.0 %all-reduce.33.cloned.1.call-start = ((), (), s32[]{:S(2)}) async-start(), calls=%async_computation.10 | async-start | bytes 524288 | tf_op jit(solution)/shard_map/psum | solution.py:25
  983.8 20.0 %collective-permute-start.9 = (f32[1024,256]{0,1:T(8,128)}, f32[1024,256]{0,1:T(8,128)}, u32[]{:S(2)}, u32[]{:S(2)}) collective-permute-start(f32[1024,256]{0,1:T(8,128)} %copy.86), channel_id=1, source_target_pairs={{0,16},{16,0},{8,24},{24,8},{32,48},{48,32},{40,56},{56,40},{64,80... | collective-permute-start | bytes 3145736 | tf_op jit(solution)/shard_map/ppermute | solution.py:20
  1016.5 182.9 %all-reduce.35.cloned.1.call-start = ((), (), s32[]{:S(2)}) async-start(), calls=%async_computation.11 | async-start | bytes 524288 | tf_op jit(solution)/shard_map/psum | solution.py:25
  1089.8 13.7 collective-permute-start.12
  1132.3 184.1 %all-reduce.37.cloned.1.call-start = ((), (), s32[]{:S(2)}) async-start(), calls=%async_computation.12 | async-start | bytes 524288 | tf_op jit(solution)/shard_map/psum | solution.py:25
  1249.3 184.1 %all-reduce.39.cloned.1.call-start = ((), (), s32[]{:S(2)}) async-start(), calls=%async_computation.13 | async-start | bytes 524288 | tf_op jit(solution)/shard_map/psum | solution.py:25
  1366.4 184.1 %all-reduce.41.cloned.1.call-start = ((), (), s32[]{:S(2)}) async-start(), calls=%async_computation.14 | async-start | bytes 524288 | tf_op jit(solution)/shard_map/psum | solution.py:25
  1441.1 13.5 collective-permute-start.18
  1483.4 184.4 %all-reduce.43.cloned.1.call-start = ((), (), s32[]{:S(2)}) async-start(), calls=%async_computation.15 | async-start | bytes 524288 | tf_op jit(solution)/shard_map/psum | solution.py:25
  1558.2 13.7 collective-permute-start.20
  1600.7 184.8 %all-reduce.45.cloned.1.call-start = ((), (), s32[]{:S(2)}) async-start(), calls=%async_computation.16 | async-start | bytes 524288 | tf_op jit(solution)/shard_map/psum | solution.py:25
  1718.4 189.3 %all-reduce.47.cloned.1.call-start = ((), (), s32[]{:S(2)}) async-start(), calls=%async_computation.17 | async-start | bytes 524288 | tf_op jit(solution)/shard_map/psum | solution.py:25
  1793.2 13.4 collective-permute-start.24
  1916.1 13.7 collective-permute-start.26
  (89 other events, 3465.6 us)
Sparse Core Ops, SparseCore 0:
  9.7 63.4 all-gather.2
  95.9 64.7 all-reduce.16
  198.7 66.9 all-reduce.18
  303.9 66.9 all-reduce.20
  408.9 67.0 all-reduce.22
  514.0 66.9 all-reduce.24
  619.1 66.9 all-reduce.26
  724.3 66.9 all-reduce.28
  829.3 66.9 all-reduce.30
  935.3 41.6 all-gather.4
  1016.6 65.5 all-reduce.32
  1132.4 66.9 all-reduce.34
  1249.4 66.9 all-reduce.36
  1366.5 66.9 all-reduce.38
  1483.5 66.9 all-reduce.40
  1600.8 66.9 all-reduce.42
  1718.6 66.9 all-reduce.44
  1840.7 66.9 all-reduce.46
where the time goes:
time: 1980 us; the launch traced here: 1970 us
  waiting for transfers between devices  1300 us (66%)
  other arithmetic  415 us (21%)
  starting transfers between devices  111 us (6%)
  local copies, waits for them, and re-layouts  86 us (4%)
  matrix products  35.7 us (2%)
    psum x16, waiting for transfers between devices, spread(): return lax.psum(block, axis)  1070 us
    another operation x48, other arithmetic, factor_panels(): chol_block = jnp.linalg.cholesky(fetched[:panel_width])  198 us
    another operation x32, other arithmetic, solve_rows(): jax.scipy.linalg.solve_triangular(chol_block, right_side.T, lower=True)  168 us
    ppermute x27, waiting for transfers between devices, swapped(): return lax.ppermute(block, axis, route)  128 us
    ppermute x27, starting transfers between devices, swapped(): return lax.ppermute(block, axis, route)  110 us
    all_gather x2, waiting for transfers between devices, assemble(): gathered = lax.all_gather(child_tile, 'front', axis=1, tiled=True)  106 us
  transfers between devices with their start and end apart: 45, of which 43 were waited for; matrix products, arithmetic and copies ran while one was open for 1% of the time, Pallas kernels for 0%

commit v1 on v0

--- a/solution.py
+++ b/solution.py
@@ -8,6 +8,16 @@
 UPD = 1024
 FR = 2048
 HIGHEST = lax.Precision.HIGHEST
+
+
+def gather_by_hops(x, axis, dim):
+    size = lax.axis_size(axis)
+    held, blocks = (x, [x])
+    for _ in range(size - 1):
+        held = lax.ppermute(held, axis, [(i, (i + 1) % size) for i in range(size)])
+        blocks.insert(0, held)
+    line = jnp.concatenate(blocks, axis=dim)
+    return jnp.roll(line, (lax.axis_index(axis) + 1) * x.shape[dim], axis=dim)
 
 
 def swapped(block, axis, stride):
@@ -69,7 +79,7 @@
     update_blocks = UPD // BLK
     front_blocks = FR // BLK
     tile_cols = 2 * col_blocks * BLK
-    gathered = lax.all_gather(child_tile, "front", axis=1, tiled=True)
+    gathered = gather_by_hops(child_tile, "front", 1)
     child_rows = gathered.shape[0]
     child_row_blocks = child_rows // BLK
     both_maps = lax.dynamic_index_in_dim(parent_map, front_group, 0, keepdims=False)

time: 1980 us -> 2040 us (1.030)
  waiting for transfers between devices: 1300 us -> 1330 us
    ppermute x0 -> x14, waiting for transfers between devices: none -> 134 us  [gather_by_hops(): held = lax.ppermute(held, axis, [(i, (i + 1) % size) for i in range(size)])]
    all_gather x2 -> x0, waiting for transfers between devices: 106 us -> none  [assemble(): gathered = lax.all_gather(child_tile, 'front', axis=1, tiled=True)]
  transfers between devices with their start and end apart: 45 -> 57, of which waited for: 43 -> 55; matrix products, arithmetic and copies ran while one was open for 1% -> 1% of each run, Pallas kernels for 0% -> 0%
where the time goes in v1:
time: 2040 us; the launch traced here: 2030 us
  waiting for transfers between devices  1330 us (65%)
  other arithmetic  423 us (21%)
  starting transfers between devices  119 us (6%)
  local copies, waits for them, and re-layouts  96.3 us (5%)
  matrix products  41.8 us (2%)
    psum x16, waiting for transfers between devices, spread(): return lax.psum(block, axis)  1070 us
    another operation x48, other arithmetic, factor_panels(): chol_block = jnp.linalg.cholesky(fetched[:panel_width])  201 us
    another operation x32, other arithmetic, solve_rows(): jax.scipy.linalg.solve_triangular(chol_block, right_side.T, lower=True)  170 us
    ppermute x14, waiting for transfers between devices, gather_by_hops(): held = lax.ppermute(held, axis, [(i, (i + 1) % size) for i in range(size)])  134 us
    ppermute x27, waiting for transfers between devices, swapped(): return lax.ppermute(block, axis, route)  125 us
    ppermute x27, starting transfers between devices, swapped(): return lax.ppermute(block, axis, route)  115 us
  transfers between devices with their start and end apart: 57, of which 55 were waited for; matrix products, arithmetic and copies ran while one was open for 1% of the time, Pallas kernels for 0%

profile of v1, /device:TPU:1, one launch (start us, length us, event | category | flops | bytes accessed | tf_op | source)
XLA Modules:
  0.0 2029.3 jit_solution(15408159403474425599)
XLA Ops:
  9.8 15.8 collective-permute-done
  25.6 13.4 collective-permute-done.1
  39.0 12.5 collective-permute-done.2
  124.0 67.2 %all-reduce.17.cloned.1.call-done = f32[1024,128]{0,1:T(8,128)} async-done(((f32[1024,128]{0,1:T(8,128)}), f32[1024,128]{0,1:T(8,128)}) %all-reduce.17.cloned.1.call-update) | async-done | bytes 524304 | tf_op jit(solution)/shard_map/psum | solution.py:35
  229.4 67.0 %all-reduce.19.cloned.1.call-done = f32[1024,128]{0,1:T(8,128)} async-done(((f32[1024,128]{0,1:T(8,128)}), f32[1024,128]{0,1:T(8,128)}) %all-reduce.19.cloned.1.call-update) | async-done | bytes 524304 | tf_op jit(solution)/shard_map/psum | solution.py:35
  334.3 67.1 %all-reduce.21.cloned.1.call-done = f32[1024,128]{0,1:T(8,128)} async-done(((f32[1024,128]{0,1:T(8,128)}), f32[1024,128]{0,1:T(8,128)}) %all-reduce.21.cloned.1.call-update) | async-done | bytes 524304 | tf_op jit(solution)/shard_map/psum | solution.py:35
  439.4 66.9 %all-reduce.23.cloned.1.call-done = f32[1024,128]{0,1:T(8,128)} async-done(((f32[1024,128]{0,1:T(8,128)}), f32[1024,128]{0,1:T(8,128)}) %all-reduce.23.cloned.1.call-update) | async-done | bytes 524304 | tf_op jit(solution)/shard_map/psum | solution.py:35
  545.2 67.0 %all-reduce.25.cloned.1.call-done = f32[1024,128]{0,1:T(8,128)} async-done(((f32[1024,128]{0,1:T(8,128)}), f32[1024,128]{0,1:T(8,128)}) %all-reduce.25.cloned.1.call-update) | async-done | bytes 524304 | tf_op jit(solution)/shard_map/psum | solution.py:35
  651.5 67.1 %all-reduce.27.cloned.1.call-done = f32[1024,128]{0,1:T(8,128)} async-done(((f32[1024,128]{0,1:T(8,128)}), f32[1024,128]{0,1:T(8,128)}) %all-reduce.27.cloned.1.call-update) | async-done | bytes 524304 | tf_op jit(solution)/shard_map/psum | solution.py:35
  757.4 67.1 %all-reduce.29.cloned.1.call-done = f32[1024,128]{0,1:T(8,128)} async-done(((f32[1024,128]{0,1:T(8,128)}), f32[1024,128]{0,1:T(8,128)}) %all-reduce.29.cloned.1.call-update) | async-done | bytes 524304 | tf_op jit(solution)/shard_map/psum | solution.py:35
  863.5 67.0 %all-reduce.31.cloned.1.call-done = f32[1024,128]{0,1:T(8,128)} async-done(((f32[1024,128]{0,1:T(8,128)}), f32[1024,128]{0,1:T(8,128)}) %all-reduce.31.cloned.1.call-update) | async-done | bytes 524304 | tf_op jit(solution)/shard_map/psum | solution.py:35
  1032.5 13.3 collective-permute-done.23
  1061.1 65.9 %all-reduce.33.cloned.1.call-done = f32[512,128]{0,1:T(8,128)} async-done(((f32[512,128]{0,1:T(8,128)}), f32[512,128]{0,1:T(8,128)}) %all-reduce.33.cloned.1.call-update) | async-done | bytes 262160 | tf_op jit(solution)/shard_map/psum | solution.py:35
  1177.0 67.0 %all-reduce.35.cloned.1.call-done = f32[512,128]{0,1:T(8,128)} async-done(((f32[512,128]{0,1:T(8,128)}), f32[512,128]{0,1:T(8,128)}) %all-reduce.35.cloned.1.call-update) | async-done | bytes 262160 | tf_op jit(solution)/shard_map/psum | solution.py:35
  1294.2 67.0 %all-reduce.37.cloned.1.call-done = f32[512,128]{0,1:T(8,128)} async-done(((f32[512,128]{0,1:T(8,128)}), f32[512,128]{0,1:T(8,128)}) %all-reduce.37.cloned.1.call-update) | async-done | bytes 262160 | tf_op jit(solution)/shard_map/psum | solution.py:35
  1370.4 11.8 collective-permute-done.30
  1411.2 67.0 %all-reduce.39.cloned.1.call-done = f32[512,128]{0,1:T(8,128)} async-done(((f32[512,128]{0,1:T(8,128)}), f32[512,128]{0,1:T(8,128)}) %all-reduce.39.cloned.1.call-update) | async-done | bytes 262160 | tf_op jit(solution)/shard_map/psum | solution.py:35
  1487.5 11.8 collective-permute-done.32
  1528.2 67.0 %all-reduce.41.cloned.1.call-done = f32[512,128]{0,1:T(8,128)} async-done(((f32[512,128]{0,1:T(8,128)}), f32[512,128]{0,1:T(8,128)}) %all-reduce.41.cloned.1.call-update) | async-done | bytes 262160 | tf_op jit(solution)/shard_map/psum | solution.py:35
  1604.6 11.8 collective-permute-done.34
  1645.3 67.0 %all-reduce.43.cloned.1.call-done = f32[512,128]{0,1:T(8,128)} async-done(((f32[512,128]{0,1:T(8,128)}), f32[512,128]{0,1:T(8,128)}) %all-reduce.43.cloned.1.call-update) | async-done | bytes 262160 | tf_op jit(solution)/shard_map/psum | solution.py:35
  1763.3 67.1 %all-reduce.45.cloned.1.call-done = f32[512,128]{0,1:T(8,128)} async-done(((f32[512,128]{0,1:T(8,128)}), f32[512,128]{0,1:T(8,128)}) %all-reduce.45.cloned.1.call-update) | async-done | bytes 262160 | tf_op jit(solution)/shard_map/psum | solution.py:35
  1864.3 13.2 cholesky.408
  1899.8 67.0 %all-reduce.47.cloned.1.call-done = f32[512,128]{0,1:T(8,128)} async-done(((f32[512,128]{0,1:T(8,128)}), f32[512,128]{0,1:T(8,128)}) %all-reduce.47.cloned.1.call-update) | async-done | bytes 262160 | tf_op jit(solution)/shard_map/psum | solution.py:35
  (693 shorter events, 836.8 us)
Async XLA Ops:
  7.2 184.0 %all-reduce.17.cloned.1.call-start = ((), (), s32[]{:S(2)}) async-start(), calls=%async_computation | async-start | bytes 1048576 | tf_op jit(solution)/shard_map/psum | solution.py:35
  7.2 18.3 collective-permute-start
  123.8 172.6 %all-reduce.19.cloned.1.call-start = ((), (), s32[]{:S(2)}) async-start(), calls=%async_computation.1 | async-start | bytes 1048576 | tf_op jit(solution)/shard_map/psum | solution.py:35
  229.3 172.1 %all-reduce.21.cloned.1.call-start = ((), (), s32[]{:S(2)}) async-start(), calls=%async_computation.2 | async-start | bytes 1048576 | tf_op jit(solution)/shard_map/psum | solution.py:35
  334.2 172.1 %all-reduce.23.cloned.1.call-start = ((), (), s32[]{:S(2)}) async-start(), calls=%async_computation.3 | async-start | bytes 1048576 | tf_op jit(solution)/shard_map/psum | solution.py:35
  439.2 173.1 %all-reduce.25.cloned.1.call-start = ((), (), s32[]{:S(2)}) async-start(), calls=%async_computation.4 | async-start | bytes 1048576 | tf_op jit(solution)/shard_map/psum | solution.py:35
  545.2 173.4 %all-reduce.27.cloned.1.call-start = ((), (), s32[]{:S(2)}) async-start(), calls=%async_computation.5 | async-start | bytes 1048576 | tf_op jit(solution)/shard_map/psum | solution.py:35
  651.4 173.1 %all-reduce.29.cloned.1.call-start = ((), (), s32[]{:S(2)}) async-start(), calls=%async_computation.6 | async-start | bytes 1048576 | tf_op jit(solution)/shard_map/psum | solution.py:35
  757.4 173.2 %all-reduce.31.cloned.1.call-start = ((), (), s32[]{:S(2)}) async-start(), calls=%async_computation.7 | async-start | bytes 1048576 | tf_op jit(solution)/shard_map/psum | solution.py:35
  863.4 263.6 %all-reduce.33.cloned.1.call-start = ((), (), s32[]{:S(2)}) async-start(), calls=%async_computation.8 | async-start | bytes 524288 | tf_op jit(solution)/shard_map/psum | solution.py:35
  1028.4 17.4 collective-permute-start.23
  1061.1 182.9 %all-reduce.35.cloned.1.call-start = ((), (), s32[]{:S(2)}) async-start(), calls=%async_computation.9 | async-start | bytes 524288 | tf_op jit(solution)/shard_map/psum | solution.py:35
  1134.7 13.4 collective-permute-start.26
  1176.9 184.3 %all-reduce.37.cloned.1.call-start = ((), (), s32[]{:S(2)}) async-start(), calls=%async_computation.10 | async-start | bytes 524288 | tf_op jit(solution)/shard_map/psum | solution.py:35
  1251.7 13.6 collective-permute-start.28
  1294.1 184.1 %all-reduce.39.cloned.1.call-start = ((), (), s32[]{:S(2)}) async-start(), calls=%async_computation.11 | async-start | bytes 524288 | tf_op jit(solution)/shard_map/psum | solution.py:35
  1411.2 184.1 %all-reduce.41.cloned.1.call-start = ((), (), s32[]{:S(2)}) async-start(), calls=%async_computation.12 | async-start | bytes 524288 | tf_op jit(solution)/shard_map/psum | solution.py:35
  1485.9 13.4 collective-permute-start.32
  1528.2 184.1 %all-reduce.43.cloned.1.call-start = ((), (), s32[]{:S(2)}) async-start(), calls=%async_computation.13 | async-start | bytes 524288 | tf_op jit(solution)/shard_map/psum | solution.py:35
  1602.9 13.5 collective-permute-start.34
  1645.3 185.1 %all-reduce.45.cloned.1.call-start = ((), (), s32[]{:S(2)}) async-start(), calls=%async_computation.14 | async-start | bytes 524288 | tf_op jit(solution)/shard_map/psum | solution.py:35
  1720.0 13.7 collective-permute-start.36
  1763.2 203.6 %all-reduce.47.cloned.1.call-start = ((), (), s32[]{:S(2)}) async-start(), calls=%async_computation.15 | async-start | bytes 524288 | tf_op jit(solution)/shard_map/psum | solution.py:35
  1975.3 13.6 collective-permute-start.40
  (99 other events, 4097.4 us)
Sparse Core Ops, SparseCore 0:
  123.9 67.1 all-reduce.16
  229.4 66.9 all-reduce.18
  334.3 67.0 all-reduce.20
  439.3 66.9 all-reduce.22
  545.3 66.9 all-reduce.24
  651.5 66.9 all-reduce.26
  757.5 66.9 all-reduce.28
  863.6 66.9 all-reduce.30
  1061.2 65.8 all-reduce.32
  1177.0 66.9 all-reduce.34
  1294.3 66.9 all-reduce.36
  1411.3 66.9 all-reduce.38
  1528.3 66.9 all-reduce.40
  1645.4 66.8 all-reduce.42
  1763.4 66.9 all-reduce.44
  1899.9 66.9 all-reduce.46
